TPU v7x, 256 devices: a whole 4x4x8 slice. The times are simulated.
256 devices in a mesh: grp: 4 (over x), own: 64 (over z, y, core).
Axes of the slice: x: 4, y: 4, z: 8, core: 2. Of those that a mesh axis runs over, the one named last changes fastest.
Arguments:
- coefficients: bfloat16 [64, 1024, 4608], P('own', 'grp'), parts along dimension 1, may hold values from -6 to 6
- rotations: bfloat16 [64, 3342336], P('own'), may hold values from -0.75 to 0.75
- legendre: bfloat16 [256, 512, 512], P('own'), may hold values from -48 to 48, as said below
- degree_slot: int32 [8, 64], replicated, may hold values from 0 to 63, each once within a row
- column_order: int32 [1024], P('grp'), parts along dimension 0, may hold values from 0 to 255, each once
Outputs:
- grid_errors: bfloat16 [1024, 256, 1024], P('grp', 'own'), parts along dimension 0
There are 4 independent parts, one for each index of `grp`. A program takes and returns all parts, laid end to end along the dimension named above; an argument that names none is the same for every part. Nothing has to cross between parts.
Inputs may be any that keep to these rules, and one draw needn't show every extreme that they name: Each row is a permutation; slot s of class k holds degree 64 * k + degree_slot[k, s]. `column_order`: a permutation of the columns. legendre[t, m, l] is zero where l < m.
All inputs are finite; a program needn't handle non-finite values.
Results may differ from a plain program's by a relative error of at most 0.0062.
Values may be sent and summed in bfloat16 or wider, within the bound.
No kernel may reach another device: no remote copies, remote signals or barrier semaphores. Data moves between devices by JAX's collectives and lax.ppermute only.
A program may use at most 128 MiB of HBM per device.

v0:
```python
import functools
import math

import jax
import jax.numpy as jnp
from jax import lax
from jax.experimental import pallas as pl
from jax.experimental.pallas import tpu as pltpu
from jax.sharding import PartitionSpec as P

SLOTS = 64
CLASSES = 8
COLUMNS = 256
ORDERS = SLOTS * CLASSES
NLON = 2 * ORDERS
PAIRED = CLASSES // 2
WIDE = 2 * COLUMNS
PACKED = PAIRED * WIDE + COLUMNS
FRONT = SLOTS * CLASSES
BF = jnp.bfloat16
F32 = jnp.float32
VMEM_LIMIT = 60 * 1024 * 1024


def extent(k):
    return 2 * SLOTS * (k + 1)


def first_row(k):
    return SLOTS * k * (k + 1)


def rotation_offset(k):
    return 4 * SLOTS * SLOTS * k * (k + 1) * (2 * k + 1) // 6


def packed_rows(group):
    if group == 0:
        return [(r, 0) for r in range(CLASSES)]
    other = CLASSES - group
    return [(r, group) if r >= group else (r + other, other) for r in range(CLASSES)]


def interleave(reverse_from):
    size = CLASSES * SLOTS
    row = lax.broadcasted_iota(jnp.int32, (size, size), 0)
    col = lax.broadcasted_iota(jnp.int32, (size, size), 1)
    d = row // CLASSES
    r = row % CLASSES
    d = jnp.where(r >= reverse_from, SLOTS - 1 - d, d)
    return jnp.where(col == r * SLOTS + d, 1.0, 0.0).astype(BF)


def rotate_kernel(deg_ref, order_ref, coef_ref, rot_ref, out_ref, *scratch):
    flats = scratch[:CLASSES]
    wide = scratch[CLASSES : CLASSES + 2]
    turned = scratch[CLASSES + 2 : CLASSES + 4]
    y_ref, sems = scratch[CLASSES + 4 :]
    own = lax.axis_index("own")
    copies = []
    for k in range(CLASSES):
        size = extent(k) * extent(k)
        copy = pltpu.make_async_copy(
            rot_ref.at[:, pl.ds(rotation_offset(k), size)], flats[k], sems.at[k]
        )
        copy.start()
        copies.append(copy)
    chosen = lax.broadcasted_iota(jnp.int32, (COLUMNS, COLUMNS), 0) == order_ref[...]
    chosen = jnp.where(chosen, 1.0, 0.0).astype(BF)
    for k in range(CLASSES):
        n = extent(k)
        rows = n * (k + 1)
        v_ref = wide[k % 2]
        r_ref = turned[k % 2]
        copies[k].wait()
        v_ref[FRONT : FRONT + rows, :] = flats[k][...].astype(F32).reshape(rows, 128)
        slot_degree = deg_ref[k, own]
        degree = SLOTS * k + slot_degree
        for j in range(k + 1):
            for p in range(2):
                start = degree + SLOTS * j if p == 0 else degree - SLOTS * j - (SLOTS - 1)
                base = FRONT + start * (k + 1)
                at = (2 * j + p) * SLOTS
                for a in range(k + 1):
                    if k == 0:
                        window = v_ref[pl.ds(base, SLOTS), :]
                    else:
                        window = v_ref[pl.ds(base + a, SLOTS, stride=k + 1), :]
                    r_ref[at : at + SLOTS, a * 128 : (a + 1) * 128] = window.astype(BF)
        block = coef_ref[:, first_row(k) : first_row(k) + n]
        lane = lax.broadcasted_iota(jnp.int32, (COLUMNS, n), 1)
        block = jnp.where(lane < 2 * degree + 1, block, jnp.zeros((), BF))
        y = lax.dot_general(
            r_ref[:n, :n], block, (((1,), (1,)), ((), ())), preferred_element_type=F32
        ).astype(BF)
        row = lax.broadcasted_iota(jnp.int32, (SLOTS, COLUMNS), 0)
        y = jnp.dot(y, chosen, preferred_element_type=F32)
        base = first_row(k)
        for j in range(k + 1):
            for p in range(2):
                at = (2 * j + p) * SLOTS
                part = y[at : at + SLOTS, :]
                order = row if p == 0 else SLOTS - 1 - row
                if j == k:
                    part = jnp.where(order <= slot_degree, part, 0.0)
                if j == 0 and p == 1:
                    part = jnp.where(order >= 1, part, 0.0)
                y_ref[base + at : base + at + SLOTS, :] = part.astype(BF)

    def piece(k, j, p):
        at = first_row(k) + (2 * j + p) * SLOTS
        return y_ref[at : at + SLOTS, :]

    for p in range(2):
        perm = interleave(CLASSES if p == 0 else 0)
        for group in range(PAIRED):
            stacked = jnp.concatenate([piece(k, j, p) for k, j in packed_rows(group)], axis=0)
            lanes = group * WIDE + p * COLUMNS
            out_ref[:, lanes : lanes + COLUMNS] = jnp.dot(
                perm, stacked, preferred_element_type=F32
            ).astype(BF)
    stacked = jnp.concatenate(
        [piece(k, PAIRED, p) for p in range(2) for k in range(PAIRED, CLASSES)], axis=0
    )
    out_ref[:, PAIRED * WIDE :] = jnp.dot(
        interleave(PAIRED), stacked, preferred_element_type=F32
    ).astype(BF)


def rotate(degree_slot, column_order, coefficients, rotations):
    scratch = [pltpu.VMEM((1, extent(k) * extent(k)), BF) for k in range(CLASSES)]
    top = extent(CLASSES - 1)
    scratch += [pltpu.VMEM((FRONT + top * CLASSES, 128), F32)] * 2
    scratch += [pltpu.VMEM((top, top), BF)] * 2
    scratch += [
        pltpu.VMEM((first_row(CLASSES), COLUMNS), BF),
        pltpu.SemaphoreType.DMA((CLASSES,)),
    ]
    return pl.pallas_call(
        rotate_kernel,
        out_shape=jax.ShapeDtypeStruct((CLASSES * SLOTS, PACKED), BF),
        in_specs=[
            pl.BlockSpec(memory_space=pltpu.SMEM),
            pl.BlockSpec(memory_space=pltpu.VMEM),
            pl.BlockSpec(memory_space=pltpu.VMEM),
            pl.BlockSpec(memory_space=pl.ANY),
        ],
        out_specs=pl.BlockSpec(memory_space=pltpu.VMEM),
        scratch_shapes=scratch,
        compiler_params=pltpu.CompilerParams(vmem_limit_bytes=VMEM_LIMIT),
        cost_estimate=pl.CostEstimate(
            flops=4 * 10**9, bytes_accessed=18 * 10**6, transcendentals=0
        ),
        name="rotate",
    )(degree_slot, column_order, coefficients, rotations)


def legendre_kernel(grp_ref, targets_ref, *refs):
    pieces = refs[:4]
    out_ref, rows_ref = refs[4:]
    for back in range(4):
        group = lax.rem(grp_ref[0] + 4 - back, 4)
        rows_ref[pl.ds(pl.multiple_of(group * SLOTS, SLOTS), SLOTS), :] = pieces[back][...]
    size = CLASSES * SLOTS

    def one_hot(which, depth):
        row = lax.broadcasted_iota(jnp.int32, (depth, size), 0)
        return jnp.where(row == targets_ref[which : which + 1, :], 1.0, 0.0).astype(BF)

    def put(at, left, right):
        out_ref[at * 4 * SLOTS : (at + 1) * 4 * SLOTS, :] = jnp.dot(
            left, right, preferred_element_type=F32
        ).astype(BF)

    main = one_hot(0, size)
    lane = lax.broadcasted_iota(jnp.int32, (4 * SLOTS, size), 1)
    for j in range(PAIRED):
        values = rows_ref[:, j * size : (j + 1) * size]
        kept = values
        if j:
            kept = jnp.where(lane >= SLOTS * j, values, jnp.zeros((), BF))
            put(PAIRED + 1 + CLASSES - j - PAIRED, values, one_hot(j, size))
        put(j, kept, main)
    values = rows_ref[:, PAIRED * size :]
    for p in range(2):
        put(PAIRED + p, values, one_hot(PAIRED + p, size // 2))


def legendre_rows(grp, targets, pieces):
    size = CLASSES * SLOTS
    return pl.pallas_call(
        legendre_kernel,
        out_shape=jax.ShapeDtypeStruct(((CLASSES + 1) * 4 * SLOTS, size), BF),
        in_specs=[pl.BlockSpec(memory_space=pltpu.SMEM)]
        + [pl.BlockSpec(memory_space=pltpu.VMEM)] * 5,
        out_specs=pl.BlockSpec(memory_space=pltpu.VMEM),
        scratch_shapes=[pltpu.VMEM((4 * SLOTS, PAIRED * size + size // 2), BF)],
        compiler_params=pltpu.CompilerParams(vmem_limit_bytes=VMEM_LIMIT),
        cost_estimate=pl.CostEstimate(flops=10**9, bytes_accessed=4 * 10**6, transcendentals=0),
        name="legendre",
    )(grp, targets, *pieces)


def synthesize_kernel(x_ref, l_ref, out_ref, f_ref):
    size = CLASSES * SLOTS
    tall = 4 * SLOTS

    def put(j, left, lanes, width, at):
        summed = jnp.dot(
            l_ref[left * tall : (left + 1) * tall, :],
            x_ref[:, lanes : lanes + width],
            preferred_element_type=F32,
        ).astype(BF)
        for g in range(4):
            f_ref[g, j * SLOTS : (j + 1) * SLOTS, at : at + width] = summed[
                g * SLOTS : (g + 1) * SLOTS, :
            ]

    for j in range(CLASSES):
        if j < PAIRED:
            put(j, j, j * WIDE, WIDE, 0)
        elif j == PAIRED:
            for p in range(2):
                put(j, PAIRED + p, PAIRED * WIDE, COLUMNS, p * COLUMNS)
        else:
            put(j, j + 1, (CLASSES - j) * WIDE, WIDE, 0)
    perm = interleave(CLASSES)
    for g in range(4):
        out_ref[:, g * WIDE : (g + 1) * WIDE] = jnp.dot(
            perm, f_ref[g], preferred_element_type=F32
        ).astype(BF)


def synthesize(packed, rows):
    size = CLASSES * SLOTS
    return pl.pallas_call(
        synthesize_kernel,
        out_shape=jax.ShapeDtypeStruct((size, 4 * WIDE), BF),
        in_specs=[pl.BlockSpec(memory_space=pltpu.VMEM)] * 2,
        out_specs=pl.BlockSpec(memory_space=pltpu.VMEM),
        scratch_shapes=[pltpu.VMEM((4, size, WIDE), BF)],
        compiler_params=pltpu.CompilerParams(vmem_limit_bytes=VMEM_LIMIT),
        cost_estimate=pl.CostEstimate(
            flops=2 * 10**9, bytes_accessed=7 * 10**6, transcendentals=0
        ),
        name="synthesize",
    )(packed, rows)


def transform_kernel(x_ref, w_ref, out_ref, y_ref):
    for g in range(4):
        total = None
        for p in range(2):
            lanes = g * WIDE + p * COLUMNS
            part = lax.dot_general(
                x_ref[:, lanes : lanes + COLUMNS],
                w_ref[p],
                (((0,), (0,)), ((), ())),
                preferred_element_type=F32,
            )
            total = part if total is None else total + part
        for i in range(NLON // 128):
            y_ref[i, pl.ds(g, COLUMNS, stride=4), :] = total[:, i * 128 : (i + 1) * 128]
    for i in range(NLON // 128):
        out_ref[:, :, i * 128 : (i + 1) * 128] = (
            y_ref[i].reshape(COLUMNS, 4, 128).astype(BF)
        )


def transform(received, wave):
    return pl.pallas_call(
        transform_kernel,
        out_shape=jax.ShapeDtypeStruct((COLUMNS, 4, NLON), BF),
        in_specs=[pl.BlockSpec(memory_space=pltpu.VMEM)] * 2,
        out_specs=pl.BlockSpec(memory_space=pltpu.VMEM),
        scratch_shapes=[pltpu.VMEM((NLON // 128, 4 * COLUMNS, 128), F32)],
        compiler_params=pltpu.CompilerParams(vmem_limit_bytes=VMEM_LIMIT),
        cost_estimate=pl.CostEstimate(
            flops=2 * 10**9, bytes_accessed=7 * 10**6, transcendentals=0
        ),
        name="transform",
    )(received, wave)


def wave_table():
    row = jnp.arange(ORDERS, dtype=jnp.int32)
    order = SLOTS * (row % CLASSES) + row // CLASSES
    longitude = jnp.arange(NLON, dtype=jnp.int32)
    angles = (order[:, None] * longitude[None, :] % NLON).astype(F32) * (2.0 * math.pi / NLON)
    return (jnp.stack([jnp.cos(angles), jnp.sin(angles)], axis=0) / ORDERS).astype(BF)


def one_hot_targets(degree_slot):
    slot_major = degree_slot.T
    row = jnp.arange(CLASSES, dtype=jnp.int32)[None, :]
    main = slot_major + SLOTS * row
    targets = [main]
    for group in range(1, PAIRED):
        other = CLASSES - group
        shifted = jnp.roll(slot_major, -other, axis=1) + SLOTS * row
        targets.append(jnp.where(row < group, shifted, -1))
    half = jnp.roll(slot_major, -PAIRED, axis=1) + SLOTS * row
    targets.append(jnp.where(row < PAIRED, half, -1))
    half = slot_major + SLOTS * (row - PAIRED)
    targets.append(jnp.where(row >= PAIRED, half, -1))
    targets += [main, main]
    return jnp.stack(targets, axis=0).reshape(CLASSES, CLASSES * SLOTS)


def pack_legendre(latitude):
    by_class = latitude.reshape(CLASSES, SLOTS, ORDERS)
    groups = [by_class[0]]
    lane = jnp.arange(ORDERS, dtype=jnp.int32)[None, :]
    for group in range(1, PAIRED):
        other = jnp.roll(by_class[CLASSES - group], SLOTS * group, axis=1)
        groups.append(jnp.where(lane < SLOTS * group, other, by_class[group]))
    groups.append(by_class[PAIRED][:, SLOTS * PAIRED :])
    return jnp.concatenate(groups, axis=1)


def local(coefficients, rotations, legendre, degree_slot, column_order):
    grp = lax.axis_index("grp")
    latitude = lax.dynamic_index_in_dim(legendre, grp, axis=0, keepdims=False)
    sent = pack_legendre(latitude).reshape(SLOTS, 2, -1)
    mine = lax.all_to_all(sent, "own", split_axis=0, concat_axis=0, tiled=True)
    pieces = [mine]
    for shift in range(1, 4):
        pieces.append(lax.ppermute(mine, "grp", [(i, (i + shift) % 4) for i in range(4)]))
    pieces = [piece.reshape(SLOTS, -1) for piece in pieces]
    rows = legendre_rows(grp.reshape(1), one_hot_targets(degree_slot), pieces)

    outgoing = rotate(
        degree_slot,
        column_order.reshape(1, -1),
        coefficients.reshape(COLUMNS, -1),
        rotations,
    )
    packed = lax.all_to_all(
        outgoing.reshape(SLOTS, CLASSES, PACKED), "own", split_axis=0, concat_axis=0, tiled=True
    )
    fourier = synthesize(packed.reshape(SLOTS * CLASSES, PACKED), rows)
    received = lax.all_to_all(
        fourier.reshape(SLOTS, CLASSES, 4 * WIDE), "own", split_axis=0, concat_axis=0, tiled=True
    )
    return transform(received.reshape(SLOTS * CLASSES, 4 * WIDE), wave_table())


def solution(mesh):
    placed = (P("own", "grp", None), P("own", None), P("own", None, None), P(), P("grp"))
    return jax.shard_map(
        local, mesh=mesh, in_specs=placed, out_specs=P("grp", "own", None), check_vma=False
    )
```

profile of v0, /device:TPU:2, one launch (start us, length us, event | category | flops | bytes accessed | tf_op | source)
XLA Modules:
  0.0 171.4 jit_solution(5583575691723520689)
XLA Ops:
  0.0 1.0 dynamic-slice_bitcast_fusion
  1.0 0.1 slice.118
  1.1 0.9 fusion.15
  2.0 0.1 slice.114
  2.0 0.9 fusion.14
  3.0 0.9 fusion.12
  3.8 0.9 fusion.10
  4.8 0.8 reshape.399
  5.6 12.1 %all-to-all-start.1 = ((bf16[64,2,1152]{2,1,0:T(2,128)(2,1)}), bf16[64,2,1152]{2,1,0:T(2,128)(2,1)S(1)}, u32[]{:S(2)}, u32[]{:S(2)}) async-start(bf16[64,2,1152]{2,1,0:T(2,128)(2,1)} %reshape.399), calls=%async_computation.1 | async-start | bytes 589824 | tf_op jit(solution)/shard_map/all_to_all | solution.py:325
  17.7 14.5 %rotate.1 = bf16[512,2304]{1,0:T(8,128)(2,1)} custom-call(s32[8,64]{1,0:T(8,128)} %deg_ref.1, s32[1,256]{1,0:T(1,128)} %bitcast.86, bf16[256,4608]{1,0:T(8,128)(2,1)} %bitcast.66, bf16[1,3342336]{1,0:T(2,128)(2,1)} %rot_ref.1), custom_call_target="tpu_custom_call" | custom-call | flops 4000000000 | bytes 18000000 | tf_op jit(solution)/shard_map/rotate/pallas_call | solution.py:139
  32.2 0.0 all-to-all-done.1
  32.2 0.0 copy-start.2
  32.2 10.5 %all-to-all-start = ((bf16[64,8,2304]{2,1,0:T(8,128)(2,1)}), bf16[64,8,2304]{2,1,0:T(8,128)(2,1)S(1)}, u32[]{:S(2)}, u32[]{:S(2)}) async-start(bf16[64,8,2304]{2,1,0:T(8,128)(2,1)} %bitcast.65), calls=%async_computation | async-start | bytes 4718592 | tf_op jit(solution)/shard_map/all_to_all | solution.py:338
  42.7 0.1 broadcast_in_dim.76
  42.8 0.7 broadcast_in_dim.74
  43.5 0.7 broadcast_in_dim.72
  44.2 0.7 broadcast_in_dim.69
  44.9 0.0 copy-start.3
  44.9 0.0 copy-done.2
  44.9 0.1 add_select_fusion.1
  45.0 0.1 copy.19
  45.1 0.1 stack.9
  45.2 0.3 copy-done.3
  45.5 0.1 copy.18
  45.6 0.7 concatenate.75
  46.3 0.1 copy.14
  46.3 0.7 concatenate.63
  47.0 0.1 copy.16
  47.1 0.7 concatenate.67
  47.8 0.5 collective-permute-start.2
  48.4 2.4 %collective-permute-start.1 = (bf16[64,2,1152]{2,1,0:T(2,128)(2,1)S(1)}, bf16[64,2,1152]{2,1,0:T(2,128)(2,1)S(1)}, u32[]{:S(2)}, u32[]{:S(2)}) collective-permute-start(bf16[64,2,1152]{2,1,0:T(2,128)(2,1)S(1)} %all-to-all-done.1), channel_id=1, source_target_pairs={{0,128},{64,192},{128,0},{192,64},{1,129},{65,193},{129,1},{193,65... | collective-permute-start | bytes 884744 | tf_op jit(solution)/shard_map/ppermute | solution.py:328
  50.8 1.8 %collective-permute-start = (bf16[64,2,1152]{2,1,0:T(2,128)(2,1)S(1)}, bf16[64,2,1152]{2,1,0:T(2,128)(2,1)S(1)}, u32[]{:S(2)}, u32[]{:S(2)}) collective-permute-start(bf16[64,2,1152]{2,1,0:T(2,128)(2,1)S(1)} %all-to-all-done.1), channel_id=1, source_target_pairs={{0,64},{64,128},{128,192},{192,0},{1,65},{65,129},{129,193},{193,1... | collective-permute-start | bytes 884744 | tf_op jit(solution)/shard_map/ppermute | solution.py:328
  52.6 0.7 copy.17
  53.3 0.8 concatenate.71
  54.1 1.2 add.143.clone
  55.4 1.4 add.145
  56.8 0.7 copy.13
  57.5 0.8 stack.8
  58.3 1.3 add_select_fusion.3
  59.7 1.3 stack.10.targets_ref
  61.0 0.7 copy.20
  61.7 0.0 collective-permute-done.2
  61.7 0.8 copy.23
  62.5 1.4 collective-permute-done.1
  63.9 0.8 copy.22
  64.6 0.2 collective-permute-done
  64.8 0.8 copy.21
  65.5 4.0 %legendre.1.l_ref = bf16[2304,512]{1,0:T(8,128)(2,1)} custom-call(s32[1]{0:T(128)} %bitcast.4.grp_ref, s32[8,512]{1,0:T(8,128)} %stack.10.targets_ref, bf16[64,2304]{1,0:T(8,128)(2,1)} %bitcast.75, bf16[64,2304]{1,0:T(8,128)(2,1)} %bitcast.78, bf16[64,2304]{1,0:T(8,128)(2,1)} %bitcast.77, bf16[64,2304]{1,0:T(8,128)(2,1)} %bitcast.76), custom_call_target="tpu_custom_call" | custom-call | flops 1000000000 | bytes 4000000 | tf_op jit(solution)/shard_map/legendre/pallas_call | solution.py:191
  69.6 29.9 %all-to-all-done = bf16[64,8,2304]{2,1,0:T(8,128)(2,1)S(1)} async-done(((bf16[64,8,2304]{2,1,0:T(8,128)(2,1)}), bf16[64,8,2304]{2,1,0:T(8,128)(2,1)S(1)}, u32[]{:S(2)}, u32[]{:S(2)}) %all-to-all-start) | async-done | bytes 2359328 | tf_op jit(solution)/shard_map/all_to_all | solution.py:338
  99.5 0.0 copy-start
  99.5 1.4 copy-done
  100.9 6.0 %synthesize.1 = bf16[512,2048]{1,0:T(8,128)(2,1)} custom-call(bf16[512,2304]{1,0:T(8,128)(2,1)} %bitcast.67, bf16[2304,512]{1,0:T(8,128)(2,1)} %legendre.1.l_ref), custom_call_target="tpu_custom_call" | custom-call | flops 2000000000 | bytes 7000000 | tf_op jit(solution)/shard_map/synthesize/pallas_call | solution.py:236
  106.9 5.6 %all-to-all-start.2 = ((bf16[64,8,2048]{2,1,0:T(8,128)(2,1)}), bf16[64,8,2048]{2,1,0:T(8,128)(2,1)S(1)}, u32[]{:S(2)}, u32[]{:S(2)}) async-start(bf16[64,8,2048]{2,1,0:T(8,128)(2,1)} %bitcast.69), calls=%async_computation.2 | async-start | bytes 4194304 | tf_op jit(solution)/shard_map/all_to_all | solution.py:342
  112.5 8.3 %fusion.8 = (f32[1,512,1024]{2,1,0:T(8,128)S(1)}, f32[1,512,1024]{2,1,0:T(8,128)S(1)}) fusion(s32[512]{0:T(512)S(1)} %fusion.20), kind=kLoop, calls=%fused_computation.12 | loop fusion | flops 7340032 | bytes 4196352 | tf_op jit(solution)/shard_map/cos | solution.py:290
  120.8 1.9 %fusion.w_ref = bf16[2,512,1024]{2,1,0:T(8,128)(2,1)} fusion(f32[1,512,1024]{2,1,0:T(8,128)S(1)} %get-tuple-element.14, f32[1,512,1024]{2,1,0:T(8,128)S(1)} %get-tuple-element.13), kind=kLoop, calls=%fused_computation.1 | loop fusion | flops 3145728 | bytes 6291456 | tf_op jit(solution)/shard_map/convert_element_type | solution.py:290
  122.7 40.9 %all-to-all-done.2 = bf16[64,8,2048]{2,1,0:T(8,128)(2,1)S(1)} async-done(((bf16[64,8,2048]{2,1,0:T(8,128)(2,1)}), bf16[64,8,2048]{2,1,0:T(8,128)(2,1)S(1)}, u32[]{:S(2)}, u32[]{:S(2)}) %all-to-all-start.2) | async-done | bytes 2097184 | tf_op jit(solution)/shard_map/all_to_all | solution.py:342
  163.6 0.0 copy-start.1
  163.6 1.3 copy-done.1
  164.9 6.5 %transform.1 = bf16[256,4,1024]{2,1,0:T(4,128)(2,1)} custom-call(bf16[512,2048]{1,0:T(8,128)(2,1)} %bitcast.68, bf16[2,512,1024]{2,1,0:T(8,128)(2,1)} %fusion.w_ref), custom_call_target="tpu_custom_call" | custom-call | flops 2000000000 | bytes 7000000 | tf_op jit(solution)/shard_map/transform/pallas_call | solution.py:271
  (29 shorter events, 0.2 us)
Async XLA Ops:
  5.6 26.6 %all-to-all-start.1 = ((bf16[64,2,1152]{2,1,0:T(2,128)(2,1)}), bf16[64,2,1152]{2,1,0:T(2,128)(2,1)S(1)}, u32[]{:S(2)}, u32[]{:S(2)}) async-start(bf16[64,2,1152]{2,1,0:T(2,128)(2,1)} %reshape.399), calls=%async_computation.1 | async-start | bytes 589824 | tf_op jit(solution)/shard_map/all_to_all | solution.py:325
  32.2 12.8 %copy-start.2 = (s32[8,64]{1,0:T(8,128)S(1)}, s32[8,64]{1,0:T(8,128)}, u32[]{:S(2)}) copy-start(s32[8,64]{1,0:T(8,128)} %deg_ref.1) | copy-start | bytes 6148
  32.2 67.3 %all-to-all-start = ((bf16[64,8,2304]{2,1,0:T(8,128)(2,1)}), bf16[64,8,2304]{2,1,0:T(8,128)(2,1)S(1)}, u32[]{:S(2)}, u32[]{:S(2)}) async-start(bf16[64,8,2304]{2,1,0:T(8,128)(2,1)} %bitcast.65), calls=%async_computation | async-start | bytes 4718592 | tf_op jit(solution)/shard_map/all_to_all | solution.py:338
  44.9 0.5 copy-start.3
  47.8 13.9 %collective-permute-start.2 = (bf16[64,2,1152]{2,1,0:T(2,128)(2,1)S(1)}, bf16[64,2,1152]{2,1,0:T(2,128)(2,1)S(1)}, u32[]{:S(2)}, u32[]{:S(2)}) collective-permute-start(bf16[64,2,1152]{2,1,0:T(2,128)(2,1)S(1)} %all-to-all-done.1), channel_id=1, source_target_pairs={{0,192},{64,0},{128,64},{192,128},{1,193},{65,1},{129,65},{193,129... | collective-permute-start | bytes 884744 | tf_op jit(solution)/shard_map/ppermute | solution.py:328
  48.4 15.5 %collective-permute-start.1 = (bf16[64,2,1152]{2,1,0:T(2,128)(2,1)S(1)}, bf16[64,2,1152]{2,1,0:T(2,128)(2,1)S(1)}, u32[]{:S(2)}, u32[]{:S(2)}) collective-permute-start(bf16[64,2,1152]{2,1,0:T(2,128)(2,1)S(1)} %all-to-all-done.1), channel_id=1, source_target_pairs={{0,128},{64,192},{128,0},{192,64},{1,129},{65,193},{129,1},{193,65... | collective-permute-start | bytes 884744 | tf_op jit(solution)/shard_map/ppermute | solution.py:328
  50.8 14.0 %collective-permute-start = (bf16[64,2,1152]{2,1,0:T(2,128)(2,1)S(1)}, bf16[64,2,1152]{2,1,0:T(2,128)(2,1)S(1)}, u32[]{:S(2)}, u32[]{:S(2)}) collective-permute-start(bf16[64,2,1152]{2,1,0:T(2,128)(2,1)S(1)} %all-to-all-done.1), channel_id=1, source_target_pairs={{0,64},{64,128},{128,192},{192,0},{1,65},{65,129},{129,193},{193,1... | collective-permute-start | bytes 884744 | tf_op jit(solution)/shard_map/ppermute | solution.py:328
  99.5 1.4 copy-start
  106.9 56.7 %all-to-all-start.2 = ((bf16[64,8,2048]{2,1,0:T(8,128)(2,1)}), bf16[64,8,2048]{2,1,0:T(8,128)(2,1)S(1)}, u32[]{:S(2)}, u32[]{:S(2)}) async-start(bf16[64,8,2048]{2,1,0:T(8,128)(2,1)} %bitcast.69), calls=%async_computation.2 | async-start | bytes 4194304 | tf_op jit(solution)/shard_map/all_to_all | solution.py:342
  163.6 1.3 copy-start.1
where the time goes:
time: 172 us; the launch traced here: 171 us
  waiting for transfers between devices  72.3 us (42%)
  starting transfers between devices  32.9 us (19%)
  Pallas kernels  31 us (18%)
  local copies, waits for them, and re-layouts  20.6 us (12%)
  other arithmetic  14.4 us (8%)
    all_to_all x1, waiting for transfers between devices, local(): lax.all_to_all(fourier.reshape(SLOTS, CLASSES, 4 * WIDE), 'own', split_ax...  40.9 us
    all_to_all x1, waiting for transfers between devices, local(): lax.all_to_all(outgoing.reshape(SLOTS, CLASSES, PACKED), 'own', split_axi...  29.9 us
    pallas_call x1, Pallas kernels, rotate(): pl.pallas_call(rotate_kernel, out_shape=jax.ShapeDtypeStruct((CLASSES * S...  14.5 us
    all_to_all x1, starting transfers between devices, local(): mine = lax.all_to_all(sent, 'own', split_axis=0, concat_axis=0, tiled=True)  12.1 us
    all_to_all x1, starting transfers between devices, local(): lax.all_to_all(outgoing.reshape(SLOTS, CLASSES, PACKED), 'own', split_axi...  10.5 us
    cos x1, other arithmetic, wave_table(): jnp.cos(angles)  8.28 us
    unnamed x13, local copies, waits for them, and re-layouts  6.9 us
    pallas_call x1, Pallas kernels, transform(): pl.pallas_call(transform_kernel, out_shape=jax.ShapeDtypeStruct((COLUMNS,...  6.47 us
  transfers between devices with their start and end apart: 6, of which 4 were waited for; matrix products, arithmetic and copies ran while one was open for 15% of the time, Pallas kernels for 11%

commit v1 on v0

v1 whole, which is shorter than its diff:
```python
import functools
import math

import jax
import jax.numpy as jnp
from jax import lax
from jax.experimental import pallas as pl
from jax.experimental.pallas import tpu as pltpu
from jax.sharding import PartitionSpec as P

SLOTS = 64
CLASSES = 8
COLUMNS = 256
ORDERS = SLOTS * CLASSES
NLON = 2 * ORDERS
PAIRED = CLASSES // 2
WIDE = 2 * COLUMNS
STEPS = 2
GROUP = 2
OUTS = 2
PACKED = PAIRED * WIDE + COLUMNS
FRONT = SLOTS * CLASSES
BLOCKS = (PAIRED * ORDERS + ORDERS // 2) // 128
BF = jnp.bfloat16
F32 = jnp.float32
MIB = 1024 * 1024


def extent(k):
    return 2 * SLOTS * (k + 1)


def first_row(k):
    return SLOTS * k * (k + 1)


def rotation_offset(k):
    return 4 * SLOTS * SLOTS * k * (k + 1) * (2 * k + 1) // 6


def packed_rows(group):
    if group == 0:
        return [(r, 0) for r in range(CLASSES)]
    other = CLASSES - group
    return [(r, group) if r >= group else (r + other, other) for r in range(CLASSES)]


def interleave(reverse_from):
    size = CLASSES * SLOTS
    row = lax.broadcasted_iota(jnp.int32, (size, size), 0)
    col = lax.broadcasted_iota(jnp.int32, (size, size), 1)
    d = row // CLASSES
    r = row % CLASSES
    d = jnp.where(r >= reverse_from, SLOTS - 1 - d, d)
    return jnp.where(col == r * SLOTS + d, 1.0, 0.0).astype(BF)


def rotate_kernel(deg_ref, coef_hbm, rot_ref, out_hbm, *scratch):
    flats = scratch[:CLASSES]
    wide = scratch[CLASSES : CLASSES + 2]
    coef_ref, y_ref, out_ref, sems = scratch[CLASSES + 2 :]
    own = lax.axis_index("own")
    copies = []
    first = pltpu.make_async_copy(coef_hbm, coef_ref, sems.at[CLASSES])
    for k in range(CLASSES):
        size = extent(k) * extent(k)
        copies.append(
            pltpu.make_async_copy(
                rot_ref.at[:, pl.ds(rotation_offset(k), size)], flats[k], sems.at[k]
            )
        )
    for at, k in enumerate(range(CLASSES)):
        copies[k].start()
        if at == 1:
            first.start()
    row = lax.broadcasted_iota(jnp.int32, (SLOTS, COLUMNS), 0)
    for at, k in enumerate(range(CLASSES)):
        n = extent(k)
        rows = n * (k + 1)
        v_ref = wide[at % 2]
        copies[k].wait()
        v_ref[FRONT : FRONT + rows, :] = flats[k][...].astype(F32).reshape(rows, 128)
        slot_degree = deg_ref[k, own]
        degree = SLOTS * k + slot_degree
        if k == 0:
            first.wait()
        block = coef_ref[:, first_row(k) : first_row(k) + n]
        lane = lax.broadcasted_iota(jnp.int32, (COLUMNS, n), 1)
        block = jnp.where(lane < 2 * degree + 1, block, jnp.zeros((), BF))
        for j0 in range(0, k + 1, GROUP):
            js = range(j0, min(k + 1, j0 + GROUP))
            halves = []
            for j in js:
                for p in range(2):
                    start = degree + SLOTS * j if p == 0 else degree - SLOTS * j - (SLOTS - 1)
                    base = FRONT + start * (k + 1)
                    if k == 0:
                        windows = [v_ref[pl.ds(base, SLOTS), :]]
                    else:
                        windows = [
                            v_ref[pl.ds(base + a, SLOTS, stride=k + 1), :] for a in range(k + 1)
                        ]
                    halves.append(jnp.concatenate([w.astype(BF) for w in windows], axis=1))
            y = lax.dot_general(
                jnp.concatenate(halves, axis=0),
                block,
                (((1,), (1,)), ((), ())),
                preferred_element_type=F32,
            )
            for j in js:
                for p in range(2):
                    row_at = (2 * (j - j0) + p) * SLOTS
                    part = y[row_at : row_at + SLOTS, :]
                    order = row if p == 0 else SLOTS - 1 - row
                    if j == k:
                        part = jnp.where(order <= slot_degree, part, 0.0)
                    if j == 0 and p == 1:
                        part = jnp.where(order >= 1, part, 0.0)
                    at = first_row(k) + (2 * j + p) * SLOTS
                    y_ref[at : at + SLOTS, :] = part

    def piece(k, j, p):
        at = first_row(k) + (2 * j + p) * SLOTS
        return y_ref[at : at + SLOTS, :].astype(BF)

    stores = []

    def send(lo, hi):
        lanes = pl.ds(lo, hi - lo)
        store = pltpu.make_async_copy(
            out_ref.at[:, lanes], out_hbm.at[:, lanes], sems.at[CLASSES + 1 + len(stores)]
        )
        store.start()
        stores.append(store)

    perms = [interleave(CLASSES), interleave(0)]
    for group in range(PAIRED):
        for p in range(2):
            stacked = jnp.concatenate([piece(k, j, p) for k, j in packed_rows(group)], axis=0)
            lanes = group * WIDE + p * COLUMNS
            out_ref[:, lanes : lanes + COLUMNS] = jnp.dot(
                perms[p], stacked, preferred_element_type=F32
            ).astype(BF)
        if group % 2:
            send((group - 1) * WIDE, (group + 1) * WIDE)
    stacked = jnp.concatenate(
        [piece(k, PAIRED, p) for p in range(2) for k in range(PAIRED, CLASSES)], axis=0
    )
    out_ref[:, PAIRED * WIDE :] = jnp.dot(
        interleave(PAIRED), stacked, preferred_element_type=F32
    ).astype(BF)
    send(PAIRED * WIDE, PACKED)
    for store in stores:
        store.wait()


def rotate(degree_slot, coefficients, rotations):
    scratch = [pltpu.VMEM((1, extent(k) * extent(k)), BF) for k in range(CLASSES)]
    top = extent(CLASSES - 1)
    scratch += [pltpu.VMEM((FRONT + top * CLASSES, 128), F32)] * 2
    scratch += [
        pltpu.VMEM((COLUMNS, first_row(CLASSES)), BF),
        pltpu.VMEM((first_row(CLASSES), COLUMNS), F32),
        pltpu.VMEM((CLASSES * SLOTS, PACKED), BF),
        pltpu.SemaphoreType.DMA((CLASSES + 4,)),
    ]
    return pl.pallas_call(
        rotate_kernel,
        out_shape=pltpu.HBM((CLASSES * SLOTS, PACKED), BF),
        in_specs=[
            pl.BlockSpec(memory_space=pltpu.SMEM),
            pl.BlockSpec(memory_space=pl.ANY),
            pl.BlockSpec(memory_space=pl.ANY),
        ],
        out_specs=pl.BlockSpec(memory_space=pltpu.HBM),
        scratch_shapes=scratch,
        compiler_params=pltpu.CompilerParams(vmem_limit_bytes=44 * MIB),
        cost_estimate=pl.CostEstimate(
            flops=4 * 10**9, bytes_accessed=18 * 10**6, transcendentals=0
        ),
        name="rotate",
    )(degree_slot, coefficients, rotations)


def scatter_kernel(grp_ref, legendre_ref, out_ref, rows_ref):
    lane = lax.broadcasted_iota(jnp.int32, (SLOTS, ORDERS), 1)

    def order_class(j):
        return legendre_ref[0, j * SLOTS : (j + 1) * SLOTS, :].astype(F32)

    def put(values, at):
        for i in range(values.shape[1] // 128):
            rows_ref[pl.ds(at + i, SLOTS, stride=BLOCKS), :] = values[:, i * 128 : (i + 1) * 128]

    for group in range(PAIRED):
        values = order_class(group)
        if group:
            other = pltpu.roll(order_class(CLASSES - group), SLOTS * group, 1)
            values = jnp.where(lane < SLOTS * group, other, values)
        put(values, group * ORDERS // 128)
    put(order_class(PAIRED)[:, SLOTS * PAIRED :], PAIRED * ORDERS // 128)
    out_ref[...] = rows_ref[...].astype(BF)


def scatter_rows(grp, legendre):
    return pl.pallas_call(
        scatter_kernel,
        grid_spec=pltpu.PrefetchScalarGridSpec(
            num_scalar_prefetch=1,
            grid=(1,),
            in_specs=[pl.BlockSpec((1, ORDERS, ORDERS), lambda i, grp: (grp[0], 0, 0))],
            out_specs=pl.BlockSpec((SLOTS * BLOCKS, 128), lambda i, grp: (0, 0)),
            scratch_shapes=[pltpu.VMEM((SLOTS * BLOCKS, 128), F32)],
        ),
        out_shape=jax.ShapeDtypeStruct((SLOTS * BLOCKS, 128), BF),
        compiler_params=pltpu.CompilerParams(vmem_limit_bytes=60 * MIB),
        name="scatter",
    )(grp, legendre)


def legendre_kernel(grp_ref, targets_ref, *refs):
    pieces = refs[:4]
    out_ref, wide_ref, rows_ref = refs[4:]
    for back in range(4):
        group = lax.rem(grp_ref[0] + 4 - back, 4)
        wide_ref[back] = pieces[back][...].astype(F32)
        for i in range(BLOCKS):
            rows_ref[
                pl.ds(pl.multiple_of(group * SLOTS, SLOTS), SLOTS), i * 128 : (i + 1) * 128
            ] = wide_ref[back, pl.ds(i, SLOTS, stride=BLOCKS), :].astype(BF)
    size = CLASSES * SLOTS

    def one_hot(which, depth):
        row = lax.broadcasted_iota(jnp.int32, (depth, size), 0)
        return jnp.where(row == targets_ref[which : which + 1, :], 1.0, 0.0).astype(BF)

    def put(at, left, right):
        out_ref[at * 4 * SLOTS : (at + 1) * 4 * SLOTS, :] = jnp.dot(
            left, right, preferred_element_type=F32
        ).astype(BF)

    main = one_hot(0, size)
    lane = lax.broadcasted_iota(jnp.int32, (4 * SLOTS, size), 1)
    for j in range(PAIRED):
        values = rows_ref[:, j * size : (j + 1) * size]
        kept = values
        if j:
            kept = jnp.where(lane >= SLOTS * j, values, jnp.zeros((), BF))
            put(CLASSES + 1 - j, values, one_hot(j, size))
        put(j, kept, main)
    values = rows_ref[:, PAIRED * size :]
    for p in range(2):
        put(PAIRED + p, values, one_hot(PAIRED + p, size // 2))


def legendre_rows(grp, targets, pieces):
    size = CLASSES * SLOTS
    return pl.pallas_call(
        legendre_kernel,
        out_shape=jax.ShapeDtypeStruct(((CLASSES + 1) * 4 * SLOTS, size), BF),
        in_specs=[pl.BlockSpec(memory_space=pltpu.SMEM)]
        + [pl.BlockSpec(memory_space=pltpu.VMEM)] * 5,
        out_specs=pl.BlockSpec(memory_space=pltpu.VMEM),
        scratch_shapes=[
            pltpu.VMEM((4, SLOTS * BLOCKS, 128), F32),
            pltpu.VMEM((4 * SLOTS, BLOCKS * 128), BF),
        ],
        compiler_params=pltpu.CompilerParams(vmem_limit_bytes=60 * MIB),
        cost_estimate=pl.CostEstimate(flops=10**9, bytes_accessed=4 * 10**6, transcendentals=0),
        name="legendre",
    )(grp, targets, *pieces)


def synthesize_kernel(x_ref, l_hbm, out_hbm, l_ref, f_ref, out_ref, sems):
    tall = 4 * SLOTS
    copies = []
    for i in range(CLASSES + 1):
        rows = pl.ds(i * tall, tall)
        copies.append(pltpu.make_async_copy(l_hbm.at[rows, :], l_ref.at[rows, :], sems.at[i]))
        copies[i].start()

    def put(j, left, lanes, width, at):
        summed = jnp.dot(
            l_ref[left * tall : (left + 1) * tall, :],
            x_ref[:, lanes : lanes + width],
            preferred_element_type=F32,
        )
        for g in range(4):
            for i in range(width // 128):
                f_ref[(g * WIDE + at) // 128 + i, pl.ds(j, SLOTS, stride=CLASSES), :] = summed[
                    g * SLOTS : (g + 1) * SLOTS, i * 128 : (i + 1) * 128
                ]

    for j in range(CLASSES):
        if j in (0, PAIRED):
            for i in range(j, PAIRED if j == 0 else CLASSES + 1):
                copies[i].wait()
        if j < PAIRED:
            put(j, j, j * WIDE, WIDE, 0)
        elif j == PAIRED:
            for p in range(2):
                put(j, PAIRED + p, PAIRED * WIDE, COLUMNS, p * COLUMNS)
        else:
            put(j, j + 1, (CLASSES - j) * WIDE, WIDE, 0)
    stores = []
    for g in range(OUTS):
        part = 4 * WIDE // OUTS
        for i in range(g * part // 128, (g + 1) * part // 128):
            out_ref[:, i * 128 : (i + 1) * 128] = f_ref[i].astype(BF)
        lanes = pl.ds(g * part, part)
        stores.append(
            pltpu.make_async_copy(
                out_ref.at[:, lanes], out_hbm.at[:, lanes], sems.at[CLASSES + 1 + g]
            )
        )
        stores[g].start()
    for store in stores:
        store.wait()


def synthesize(packed, rows):
    size = CLASSES * SLOTS
    return pl.pallas_call(
        synthesize_kernel,
        out_shape=pltpu.HBM((size, 4 * WIDE), BF),
        in_specs=[
            pl.BlockSpec(memory_space=pltpu.VMEM),
            pl.BlockSpec(memory_space=pltpu.HBM),
        ],
        out_specs=pl.BlockSpec(memory_space=pltpu.HBM),
        scratch_shapes=[
            pltpu.VMEM(rows.shape, BF),
            pltpu.VMEM((4 * WIDE // 128, size, 128), F32),
            pltpu.VMEM((size, 4 * WIDE), BF),
            pltpu.SemaphoreType.DMA((CLASSES + 5,)),
        ],
        compiler_params=pltpu.CompilerParams(vmem_limit_bytes=16 * MIB),
        cost_estimate=pl.CostEstimate(
            flops=2 * 10**9, bytes_accessed=7 * 10**6, transcendentals=0
        ),
        name="synthesize",
    )(
        packed,
        pltpu.with_memory_space_constraint(rows, pltpu.HBM),
    )


def transform_kernel(order_ref, x_ref, w_hbm, out_hbm, w_ref, lhs_ref, y_ref, out_ref, sems):
    width = NLON // STEPS
    waves = []
    for i in range(STEPS):
        lanes = pl.ds(i * width, width)
        waves.append(
            pltpu.make_async_copy(w_hbm.at[:, lanes], w_ref.at[:, lanes], sems.at[i])
        )
        waves[i].start()
    chosen = lax.broadcasted_iota(jnp.int32, (COLUMNS, COLUMNS), 1) == order_ref[...]
    chosen = jnp.where(chosen, 1.0, 0.0).astype(BF)
    for g in range(4):
        for p in range(2):
            lanes = g * WIDE + p * COLUMNS
            lhs_ref[g * COLUMNS : (g + 1) * COLUMNS, p * ORDERS : (p + 1) * ORDERS] = (
                lax.dot_general(
                    chosen,
                    x_ref[:, lanes : lanes + COLUMNS],
                    (((1,), (1,)), ((), ())),
                    preferred_element_type=F32,
                ).astype(BF)
            )
    stores = []
    for step in range(STEPS):
        waves[step].wait()
        total = jnp.dot(
            lhs_ref[...],
            w_ref[:, step * width : (step + 1) * width],
            preferred_element_type=F32,
        )
        for i in range(width // 128):
            at = step * width + i * 128
            for g in range(4):
                y_ref[step % 2, i, pl.ds(g, COLUMNS, stride=4), :] = total[
                    g * COLUMNS : (g + 1) * COLUMNS, i * 128 : (i + 1) * 128
                ]
            out_ref[:, :, at : at + 128] = (
                y_ref[step % 2, i].reshape(COLUMNS, 4, 128).astype(BF)
            )
        lanes = pl.ds(step * width, width)
        stores.append(
            pltpu.make_async_copy(
                out_ref.at[:, :, lanes], out_hbm.at[:, :, lanes], sems.at[STEPS + step]
            )
        )
        stores[step].start()
    for store in stores:
        store.wait()


def transform(column_order, received, wave):
    width = NLON // STEPS
    return pl.pallas_call(
        transform_kernel,
        out_shape=pltpu.HBM((COLUMNS, 4, NLON), BF),
        in_specs=[
            pl.BlockSpec(memory_space=pltpu.VMEM),
            pl.BlockSpec(memory_space=pltpu.VMEM),
            pl.BlockSpec(memory_space=pltpu.HBM),
        ],
        out_specs=pl.BlockSpec(memory_space=pltpu.HBM),
        scratch_shapes=[
            pltpu.VMEM(wave.shape, BF),
            pltpu.VMEM((4 * COLUMNS, 2 * ORDERS), BF),
            pltpu.VMEM((2, width // 128, 4 * COLUMNS, 128), F32),
            pltpu.VMEM((COLUMNS, 4, NLON), BF),
            pltpu.SemaphoreType.DMA((2 * STEPS,)),
        ],
        compiler_params=pltpu.CompilerParams(vmem_limit_bytes=20 * MIB),
        cost_estimate=pl.CostEstimate(
            flops=2 * 10**9, bytes_accessed=7 * 10**6, transcendentals=0
        ),
        name="transform",
    )(column_order, received, pltpu.with_memory_space_constraint(wave, pltpu.HBM))


def wave_table():
    row = jnp.arange(ORDERS, dtype=jnp.int32)
    order = SLOTS * (row % CLASSES) + row // CLASSES
    longitude = jnp.arange(NLON, dtype=jnp.int32)
    angles = (order[:, None] * longitude[None, :] % NLON).astype(F32) * (2.0 * math.pi / NLON)
    return (jnp.concatenate([jnp.cos(angles), jnp.sin(angles)], axis=0) / ORDERS).astype(BF)


def one_hot_targets(degree_slot):
    slot_major = degree_slot.T
    row = jnp.arange(CLASSES, dtype=jnp.int32)[None, :]
    main = slot_major + SLOTS * row
    targets = [main]
    for group in range(1, PAIRED):
        shifted = jnp.roll(slot_major, group - CLASSES, axis=1) + SLOTS * row
        targets.append(jnp.where(row < group, shifted, -1))
    half = jnp.roll(slot_major, -PAIRED, axis=1) + SLOTS * row
    targets.append(jnp.where(row < PAIRED, half, -1))
    half = slot_major + SLOTS * (row - PAIRED)
    targets.append(jnp.where(row >= PAIRED, half, -1))
    targets += [main, main]
    return jnp.stack(targets, axis=0).reshape(CLASSES, CLASSES * SLOTS)


def local(coefficients, rotations, legendre, degree_slot, column_order):
    grp = lax.axis_index("grp")
    sent = scatter_rows(grp.reshape(1), legendre).reshape(SLOTS, BLOCKS // 2, 2, 128)
    mine = lax.all_to_all(sent, "own", split_axis=0, concat_axis=0, tiled=True)
    pieces = [mine]
    for shift in range(1, 4):
        pieces.append(lax.ppermute(mine, "grp", [(i, (i + shift) % 4) for i in range(4)]))
    pieces = [piece.reshape(SLOTS * BLOCKS, 128) for piece in pieces]
    rows = legendre_rows(grp.reshape(1), one_hot_targets(degree_slot), pieces)

    outgoing = rotate(
        degree_slot, coefficients.reshape(COLUMNS, -1), rotations
    )
    packed = lax.all_to_all(
        outgoing.reshape(SLOTS, CLASSES, PACKED), "own", split_axis=0, concat_axis=0, tiled=True
    )
    fourier = synthesize(packed.reshape(SLOTS * CLASSES, PACKED), rows)
    received = lax.all_to_all(
        fourier.reshape(SLOTS, CLASSES, 4 * WIDE), "own", split_axis=0, concat_axis=0, tiled=True
    )
    return transform(
        column_order.reshape(-1, 1), received.reshape(SLOTS * CLASSES, 4 * WIDE), wave_table()
    )


def solution(mesh):
    placed = (P("own", "grp", None), P("own", None), P("own", None, None), P(), P("grp"))
    return jax.shard_map(
        local, mesh=mesh, in_specs=placed, out_specs=P("grp", "own", None), check_vma=False
    )
```

time: 172 us -> 160 us (0.930)
  local copies, waits for them, and re-layouts: 20.6 us -> 2.39 us
  waiting for transfers between devices: 72.3 us -> 89 us
  other arithmetic: 14.4 us -> 10.4 us
  Pallas kernels: 31 us -> 27.5 us
  starting transfers between devices: 32.9 us -> 29.8 us
    ppermute x3, waiting for transfers between devices: 1.54 us -> 11.5 us  [local(): lax.ppermute(mine, 'grp', [(i, (i + shift) % 4) for i in range(4)])]
    unnamed x13 -> x12, local copies, waits for them, and re-layouts: 6.9 us -> 0.02 us
    all_to_all x1, waiting for transfers between devices: 29.9 us -> 33.7 us  [local(): lax.all_to_all(outgoing.reshape(SLOTS, CLASSES, PACKED), 'own', split_axi...]
    pallas_call x3 -> x4, Pallas kernels: 27 us -> 23.1 us  [the longest x1 10.6 us: rotate(): pl.pallas_call(rotate_kernel, out_shape=pltpu.HBM((CLASSES * SLOTS, PACKE...]
    add x3, local copies, waits for them, and re-layouts: 3.36 us -> 0.18 us  [one_hot_targets(): main = slot_major + SLOTS * row]
    all_to_all x1, starting transfers between devices: 10.5 us -> 7.59 us  [local(): lax.all_to_all(outgoing.reshape(SLOTS, CLASSES, PACKED), 'own', split_axi...]
    all_to_all x1, waiting for transfers between devices: 0.01 us -> 2.75 us  [local(): mine = lax.all_to_all(sent, 'own', split_axis=0, concat_axis=0, tiled=True)]
    unnamed x3 -> x0, other arithmetic: 2.73 us -> none
  transfers between devices with their start and end apart: 6 -> 6, of which waited for: 4 -> 6; matrix products, arithmetic and copies ran while one was open for 15% -> 8% of each run, Pallas kernels for 11% -> 9%
where the time goes in v1:
time: 160 us; the launch traced here: 159 us
  waiting for transfers between devices  89 us (56%)
  starting transfers between devices  29.8 us (19%)
  Pallas kernels  27.5 us (17%)
  other arithmetic  10.4 us (6%)
  local copies, waits for them, and re-layouts  2.39 us (1%)
    all_to_all x1, waiting for transfers between devices, local(): lax.all_to_all(fourier.reshape(SLOTS, CLASSES, 4 * WIDE), 'own', split_ax...  41 us
    all_to_all x1, waiting for transfers between devices, local(): lax.all_to_all(outgoing.reshape(SLOTS, CLASSES, PACKED), 'own', split_axi...  33.7 us
    all_to_all x1, starting transfers between devices, local(): mine = lax.all_to_all(sent, 'own', split_axis=0, concat_axis=0, tiled=True)  12.1 us
    ppermute x3, waiting for transfers between devices, local(): lax.ppermute(mine, 'grp', [(i, (i + shift) % 4) for i in range(4)])  11.5 us
    pallas_call x1, Pallas kernels, rotate(): pl.pallas_call(rotate_kernel, out_shape=pltpu.HBM((CLASSES * SLOTS, PACKE...  10.6 us
    cos x1, other arithmetic, wave_table(): jnp.cos(angles)  8.28 us
    all_to_all x1, starting transfers between devices, local(): lax.all_to_all(outgoing.reshape(SLOTS, CLASSES, PACKED), 'own', split_axi...  7.59 us
    pallas_call x1, Pallas kernels, transform(): pl.pallas_call(transform_kernel, out_shape=pltpu.HBM((COLUMNS, 4, NLON),...  5.89 us
  transfers between devices with their start and end apart: 6, of which 6 were waited for; matrix products, arithmetic and copies ran while one was open for 8% of the time, Pallas kernels for 9%

profile of v1, /device:TPU:2, one launch (start us, length us, event | category | flops | bytes accessed | tf_op | source)
XLA Modules:
  0.0 159.5 jit_solution(7127947540707598085)
XLA Ops:
  0.0 0.0 copy-start.1
  0.0 0.0 copy-start
  0.0 2.0 %scatter.1 = bf16[1152,128]{1,0:T(8,128)(2,1)} custom-call(s32[1]{0:T(128)} %bitcast.4.grp_ref, bf16[4,512,512]{2,1,0:T(8,128)(2,1)} %legendre_ref.1), custom_call_target="tpu_custom_call" | custom-call | tf_op jit(solution)/shard_map/scatter/pallas_call | solution.py:206
  2.0 12.1 %all-to-all-start.1 = ((bf16[64,9,2,128]{3,2,1,0:T(2,128)(2,1)}), bf16[64,9,2,128]{3,2,1,0:T(2,128)(2,1)S(1)}, u32[]{:S(2)}, u32[]{:S(2)}) async-start(bf16[64,9,2,128]{3,2,1,0:T(2,128)(2,1)} %bitcast.43), calls=%async_computation.1 | async-start | bytes 589824 | tf_op jit(solution)/shard_map/all_to_all | solution.py:451
  14.1 0.0 copy-done.1
  14.2 0.0 copy-done
  14.2 10.6 %rotate.1 = bf16[512,2304]{1,0:T(8,128)(2,1)} custom-call(s32[8,64]{1,0:T(8,128)S(1)} %copy-done.1, bf16[256,4608]{1,0:T(8,128)(2,1)S(1)} %bitcast.31, bf16[1,3342336]{1,0:T(2,128)(2,1)} %rot_ref.1), custom_call_target="tpu_custom_call" | custom-call | flops 4000000000 | bytes 18000000 | tf_op jit(solution)/shard_map/rotate/pallas_call | solution.py:167
  24.8 2.7 %all-to-all-done.1 = bf16[64,9,2,128]{3,2,1,0:T(2,128)(2,1)S(1)} async-done(((bf16[64,9,2,128]{3,2,1,0:T(2,128)(2,1)}), bf16[64,9,2,128]{3,2,1,0:T(2,128)(2,1)S(1)}, u32[]{:S(2)}, u32[]{:S(2)}) %all-to-all-start.1) | async-done | bytes 294944 | tf_op jit(solution)/shard_map/all_to_all | solution.py:451
  27.6 0.0 copy-start.2
  27.6 7.6 %all-to-all-start = ((bf16[64,8,2304]{2,1,0:T(8,128)(2,1)}), bf16[64,8,2304]{2,1,0:T(8,128)(2,1)S(1)}, u32[]{:S(2)}, u32[]{:S(2)}) async-start(bf16[64,8,2304]{2,1,0:T(8,128)(2,1)} %bitcast.41), calls=%async_computation | async-start | bytes 4718592 | tf_op jit(solution)/shard_map/all_to_all | solution.py:461
  35.2 0.1 copy.18
  35.3 0.1 concatenate.63
  35.4 0.1 copy.17
  35.5 0.1 concatenate.59
  35.6 0.1 copy.16
  35.7 0.1 concatenate.55
  35.8 0.1 copy.14
  35.9 0.1 concatenate.51
  36.0 0.1 add.130
  36.1 0.1 broadcast_in_dim.50
  36.3 0.1 broadcast_in_dim.53
  36.4 0.1 broadcast_in_dim.55
  36.5 0.1 add_select_fusion.1
  36.6 1.5 collective-permute-start
  38.1 1.1 collective-permute-start.1
  39.2 0.0 copy-done.2
  39.2 2.2 %collective-permute-start.2 = (bf16[64,9,2,128]{3,2,1,0:T(2,128)(2,1)S(1)}, bf16[64,9,2,128]{3,2,1,0:T(2,128)(2,1)}, u32[]{:S(2)}, u32[]{:S(2)}) collective-permute-start(bf16[64,9,2,128]{3,2,1,0:T(2,128)(2,1)S(1)} %all-to-all-done.1), channel_id=1, source_target_pairs={{0,192},{64,0},{128,64},{192,128},{1,193},{65,1},{129,65},{193,129... | collective-permute-start | bytes 884744 | tf_op jit(solution)/shard_map/ppermute | solution.py:454
  41.3 0.1 broadcast_in_dim.57
  41.4 0.1 copy.13
  41.5 0.1 stack.6
  41.6 0.1 copy.19
  41.7 0.1 stack.7
  41.8 0.6 stack.8.targets_ref
  42.5 4.0 %collective-permute-done = bf16[64,9,2,128]{3,2,1,0:T(2,128)(2,1)S(1)} collective-permute-done((bf16[64,9,2,128]{3,2,1,0:T(2,128)(2,1)S(1)}, bf16[64,9,2,128]{3,2,1,0:T(2,128)(2,1)S(1)}, u32[]{:S(2)}, u32[]{:S(2)}) %collective-permute-start) | collective-permute-done | bytes 294944 | tf_op jit(solution)/shard_map/ppermute | solution.py:454
  46.5 0.0 copy-start.4
  46.5 3.0 %collective-permute-done.1 = bf16[64,9,2,128]{3,2,1,0:T(2,128)(2,1)S(1)} collective-permute-done((bf16[64,9,2,128]{3,2,1,0:T(2,128)(2,1)S(1)}, bf16[64,9,2,128]{3,2,1,0:T(2,128)(2,1)S(1)}, u32[]{:S(2)}, u32[]{:S(2)}) %collective-permute-start.1) | collective-permute-done | bytes 294944 | tf_op jit(solution)/shard_map/ppermute | solution.py:454
  49.4 0.0 copy-start.5
  49.4 4.6 %collective-permute-done.2 = bf16[64,9,2,128]{3,2,1,0:T(2,128)(2,1)} collective-permute-done((bf16[64,9,2,128]{3,2,1,0:T(2,128)(2,1)S(1)}, bf16[64,9,2,128]{3,2,1,0:T(2,128)(2,1)}, u32[]{:S(2)}, u32[]{:S(2)}) %collective-permute-start.2) | collective-permute-done | bytes 294944 | tf_op jit(solution)/shard_map/ppermute | solution.py:454
  54.0 0.0 copy-done.4
  54.0 0.0 copy-done.5
  54.0 4.4 %legendre.1.l_hbm = bf16[2304,512]{1,0:T(8,128)(2,1)} custom-call(s32[1]{0:T(128)} %bitcast.4.grp_ref, s32[8,512]{1,0:T(8,128)} %stack.8.targets_ref, bf16[1152,128]{1,0:T(8,128)(2,1)} %bitcast.44, bf16[1152,128]{1,0:T(8,128)(2,1)} %bitcast.46, bf16[1152,128]{1,0:T(8,128)(2,1)} %bitcast.47, bf16[1152,128]{1,0:T(8,128)(2,1)} %bitcast.18.refs_3_), custom_call_target="tpu_custom_call" | custom-call | flops 1000000000 | bytes 4000000 | tf_op jit(solution)/shard_map/legendre/pallas_call | solution.py:258
  58.4 33.7 %all-to-all-done = bf16[64,8,2304]{2,1,0:T(8,128)(2,1)S(1)} async-done(((bf16[64,8,2304]{2,1,0:T(8,128)(2,1)}), bf16[64,8,2304]{2,1,0:T(8,128)(2,1)S(1)}, u32[]{:S(2)}, u32[]{:S(2)}) %all-to-all-start) | async-done | bytes 2359328 | tf_op jit(solution)/shard_map/all_to_all | solution.py:461
  92.1 4.6 %synthesize.1 = bf16[512,2048]{1,0:T(8,128)(2,1)} custom-call(bf16[512,2304]{1,0:T(8,128)(2,1)S(1)} %bitcast.32, bf16[2304,512]{1,0:T(8,128)(2,1)} %legendre.1.l_hbm), custom_call_target="tpu_custom_call" | custom-call | flops 2000000000 | bytes 7000000 | tf_op jit(solution)/shard_map/synthesize/pallas_call | solution.py:323
  96.7 0.0 copy-start.3
  96.7 5.4 %all-to-all-start.2 = ((bf16[64,8,2048]{2,1,0:T(8,128)(2,1)}), bf16[64,8,2048]{2,1,0:T(8,128)(2,1)S(1)}, u32[]{:S(2)}, u32[]{:S(2)}) async-start(bf16[64,8,2048]{2,1,0:T(8,128)(2,1)} %bitcast.42), calls=%async_computation.2 | async-start | bytes 4194304 | tf_op jit(solution)/shard_map/all_to_all | solution.py:465
  102.1 0.0 copy-done.3
  102.1 0.1 copy.20.order_ref
  102.2 8.3 %fusion.8 = (f32[512,1024]{1,0:T(8,128)S(1)}, f32[512,1024]{1,0:T(8,128)S(1)}) fusion(s32[512]{0:T(512)S(1)} %fusion.13), kind=kLoop, calls=%fused_computation.12 | loop fusion | flops 7340032 | bytes 4196352 | tf_op jit(solution)/shard_map/cos | solution.py:429
  110.5 1.9 %fusion.w_hbm = bf16[1024,1024]{1,0:T(8,128)(2,1)} fusion(f32[512,1024]{1,0:T(8,128)S(1)} %get-tuple-element.10, f32[512,1024]{1,0:T(8,128)S(1)} %get-tuple-element.9), kind=kLoop, calls=%fused_computation.1 | loop fusion | flops 3145728 | bytes 6291456 | tf_op jit(solution)/shard_map/convert_element_type | solution.py:429
  112.5 41.0 %all-to-all-done.2 = bf16[64,8,2048]{2,1,0:T(8,128)(2,1)S(1)} async-done(((bf16[64,8,2048]{2,1,0:T(8,128)(2,1)}), bf16[64,8,2048]{2,1,0:T(8,128)(2,1)S(1)}, u32[]{:S(2)}, u32[]{:S(2)}) %all-to-all-start.2) | async-done | bytes 2097184 | tf_op jit(solution)/shard_map/all_to_all | solution.py:465
  153.4 5.9 %transform.1 = bf16[256,4,1024]{2,1,0:T(4,128)(2,1)} custom-call(s32[256,1]{1,0:T(8,128)S(1)} %copy.20.order_ref, bf16[512,2048]{1,0:T(8,128)(2,1)S(1)} %bitcast.33, bf16[1024,1024]{1,0:T(8,128)(2,1)} %fusion.w_hbm), custom_call_target="tpu_custom_call" | custom-call | flops 2000000000 | bytes 7000000 | tf_op jit(solution)/shard_map/transform/pallas_call | solution.py:400
  (24 shorter events, 0.2 us)
Async XLA Ops:
  0.0 14.1 %copy-start.1 = (s32[8,64]{1,0:T(8,128)S(1)}, s32[8,64]{1,0:T(8,128)}, u32[]{:S(2)}) copy-start(s32[8,64]{1,0:T(8,128)} %deg_ref.1) | copy-start | bytes 6148
  0.0 14.2 %copy-start = (bf16[1,256,4608]{2,1,0:T(8,128)(2,1)S(1)}, bf16[1,256,4608]{2,1,0:T(8,128)(2,1)}, u32[]{:S(2)}) copy-start(bf16[1,256,4608]{2,1,0:T(8,128)(2,1)} %param.5) | copy-start | bytes 7077892
  2.0 25.5 %all-to-all-start.1 = ((bf16[64,9,2,128]{3,2,1,0:T(2,128)(2,1)}), bf16[64,9,2,128]{3,2,1,0:T(2,128)(2,1)S(1)}, u32[]{:S(2)}, u32[]{:S(2)}) async-start(bf16[64,9,2,128]{3,2,1,0:T(2,128)(2,1)} %bitcast.43), calls=%async_computation.1 | async-start | bytes 589824 | tf_op jit(solution)/shard_map/all_to_all | solution.py:451
  27.6 11.6 %copy-start.2 = (bf16[64,9,2,128]{3,2,1,0:T(2,128)(2,1)}, bf16[64,9,2,128]{3,2,1,0:T(2,128)(2,1)S(1)}, u32[]{:S(2)}) copy-start(bf16[64,9,2,128]{3,2,1,0:T(2,128)(2,1)S(1)} %all-to-all-done.1) | copy-start | bytes 884740
  27.6 64.5 %all-to-all-start = ((bf16[64,8,2304]{2,1,0:T(8,128)(2,1)}), bf16[64,8,2304]{2,1,0:T(8,128)(2,1)S(1)}, u32[]{:S(2)}, u32[]{:S(2)}) async-start(bf16[64,8,2304]{2,1,0:T(8,128)(2,1)} %bitcast.41), calls=%async_computation | async-start | bytes 4718592 | tf_op jit(solution)/shard_map/all_to_all | solution.py:461
  36.6 9.9 %collective-permute-start = (bf16[64,9,2,128]{3,2,1,0:T(2,128)(2,1)S(1)}, bf16[64,9,2,128]{3,2,1,0:T(2,128)(2,1)S(1)}, u32[]{:S(2)}, u32[]{:S(2)}) collective-permute-start(bf16[64,9,2,128]{3,2,1,0:T(2,128)(2,1)S(1)} %all-to-all-done.1), channel_id=1, source_target_pairs={{0,64},{64,128},{128,192},{192,0},{1,65},{65,129},{129,193},{193,1... | collective-permute-start | bytes 884744 | tf_op jit(solution)/shard_map/ppermute | solution.py:454
  38.1 11.4 %collective-permute-start.1 = (bf16[64,9,2,128]{3,2,1,0:T(2,128)(2,1)S(1)}, bf16[64,9,2,128]{3,2,1,0:T(2,128)(2,1)S(1)}, u32[]{:S(2)}, u32[]{:S(2)}) collective-permute-start(bf16[64,9,2,128]{3,2,1,0:T(2,128)(2,1)S(1)} %all-to-all-done.1), channel_id=1, source_target_pairs={{0,128},{64,192},{128,0},{192,64},{1,129},{65,193},{129,1},{193,65... | collective-permute-start | bytes 884744 | tf_op jit(solution)/shard_map/ppermute | solution.py:454
  39.2 14.8 %collective-permute-start.2 = (bf16[64,9,2,128]{3,2,1,0:T(2,128)(2,1)S(1)}, bf16[64,9,2,128]{3,2,1,0:T(2,128)(2,1)}, u32[]{:S(2)}, u32[]{:S(2)}) collective-permute-start(bf16[64,9,2,128]{3,2,1,0:T(2,128)(2,1)S(1)} %all-to-all-done.1), channel_id=1, source_target_pairs={{0,192},{64,0},{128,64},{192,128},{1,193},{65,1},{129,65},{193,129... | collective-permute-start | bytes 884744 | tf_op jit(solution)/shard_map/ppermute | solution.py:454
  46.5 7.5 %copy-start.4 = (bf16[64,9,2,128]{3,2,1,0:T(2,128)(2,1)}, bf16[64,9,2,128]{3,2,1,0:T(2,128)(2,1)S(1)}, u32[]{:S(2)}) copy-start(bf16[64,9,2,128]{3,2,1,0:T(2,128)(2,1)S(1)} %collective-permute-done) | copy-start | bytes 884740
  49.4 4.6 %copy-start.5 = (bf16[64,9,2,128]{3,2,1,0:T(2,128)(2,1)}, bf16[64,9,2,128]{3,2,1,0:T(2,128)(2,1)S(1)}, u32[]{:S(2)}) copy-start(bf16[64,9,2,128]{3,2,1,0:T(2,128)(2,1)S(1)} %collective-permute-done.1) | copy-start | bytes 884740
  96.7 5.4 %copy-start.3 = (s32[256]{0:T(256)S(1)}, s32[256]{0:T(256)}, u32[]{:S(2)}) copy-start(s32[256]{0:T(256)} %param.9) | copy-start | bytes 3076
  96.7 56.7 %all-to-all-start.2 = ((bf16[64,8,2048]{2,1,0:T(8,128)(2,1)}), bf16[64,8,2048]{2,1,0:T(8,128)(2,1)S(1)}, u32[]{:S(2)}, u32[]{:S(2)}) async-start(bf16[64,8,2048]{2,1,0:T(8,128)(2,1)} %bitcast.42), calls=%async_computation.2 | async-start | bytes 4194304 | tf_op jit(solution)/shard_map/all_to_all | solution.py:465

commit v2 on v1

--- a/solution.py
+++ b/solution.py
@@ -17,7 +17,8 @@
 WIDE = 2 * COLUMNS
 STEPS = 2
 GROUP = 2
-OUTS = 2
+OUTS = 4
+WAITS = {0: (0, 1), 2: (2, 3, 4)}
 PACKED = PAIRED * WIDE + COLUMNS
 FRONT = SLOTS * CLASSES
 BLOCKS = (PAIRED * ORDERS + ORDERS // 2) // 128
@@ -74,19 +75,21 @@
         if at == 1:
             first.start()
     row = lax.broadcasted_iota(jnp.int32, (SLOTS, COLUMNS), 0)
+    lane = lax.broadcasted_iota(jnp.int32, (COLUMNS, 128), 1)
     for at, k in enumerate(range(CLASSES)):
         n = extent(k)
         rows = n * (k + 1)
         v_ref = wide[at % 2]
         copies[k].wait()
-        v_ref[FRONT : FRONT + rows, :] = flats[k][...].astype(F32).reshape(rows, 128)
+        v_ref[FRONT : FRONT + rows, :] = flats[k][...].reshape(rows, 128).astype(F32)
         slot_degree = deg_ref[k, own]
         degree = SLOTS * k + slot_degree
         if k == 0:
             first.wait()
-        block = coef_ref[:, first_row(k) : first_row(k) + n]
-        lane = lax.broadcasted_iota(jnp.int32, (COLUMNS, n), 1)
-        block = jnp.where(lane < 2 * degree + 1, block, jnp.zeros((), BF))
+        tail = pl.ds(first_row(k) + n - 128, 128)
+        coef_ref[:, tail] = jnp.where(
+            lane < 2 * slot_degree + 1, coef_ref[:, tail], jnp.zeros((), BF)
+        )
         for j0 in range(0, k + 1, GROUP):
             js = range(j0, min(k + 1, j0 + GROUP))
             halves = []
@@ -103,7 +106,7 @@
                     halves.append(jnp.concatenate([w.astype(BF) for w in windows], axis=1))
             y = lax.dot_general(
                 jnp.concatenate(halves, axis=0),
-                block,
+                coef_ref[:, first_row(k) : first_row(k) + n],
                 (((1,), (1,)), ((), ())),
                 preferred_element_type=F32,
             )
@@ -234,30 +237,30 @@
         row = lax.broadcasted_iota(jnp.int32, (depth, size), 0)
         return jnp.where(row == targets_ref[which : which + 1, :], 1.0, 0.0).astype(BF)
 
-    def put(at, left, right):
-        out_ref[at * 4 * SLOTS : (at + 1) * 4 * SLOTS, :] = jnp.dot(
-            left, right, preferred_element_type=F32
-        ).astype(BF)
+    def picked(left, right):
+        return jnp.dot(left, right, preferred_element_type=F32)
 
     main = one_hot(0, size)
     lane = lax.broadcasted_iota(jnp.int32, (4 * SLOTS, size), 1)
-    for j in range(PAIRED):
-        values = rows_ref[:, j * size : (j + 1) * size]
-        kept = values
-        if j:
-            kept = jnp.where(lane >= SLOTS * j, values, jnp.zeros((), BF))
-            put(CLASSES + 1 - j, values, one_hot(j, size))
-        put(j, kept, main)
-    values = rows_ref[:, PAIRED * size :]
-    for p in range(2):
-        put(PAIRED + p, values, one_hot(PAIRED + p, size // 2))
+    for group in range(PAIRED + 1):
+        values = rows_ref[:, group * size : group * size + (size if group < PAIRED else size // 2)]
+        if group == 0:
+            merged = picked(values, main)
+        elif group < PAIRED:
+            kept = jnp.where(lane >= SLOTS * group, values, jnp.zeros((), BF))
+            merged = picked(kept, main) + picked(values, one_hot(group, size))
+        else:
+            merged = picked(values, one_hot(PAIRED, size // 2)) + picked(
+                values, one_hot(PAIRED + 1, size // 2)
+            )
+        out_ref[group * 4 * SLOTS : (group + 1) * 4 * SLOTS, :] = merged.astype(BF)
 
 
 def legendre_rows(grp, targets, pieces):
     size = CLASSES * SLOTS
     return pl.pallas_call(
         legendre_kernel,
-        out_shape=jax.ShapeDtypeStruct(((CLASSES + 1) * 4 * SLOTS, size), BF),
+        out_shape=jax.ShapeDtypeStruct(((PAIRED + 1) * 4 * SLOTS, size), BF),
         in_specs=[pl.BlockSpec(memory_space=pltpu.SMEM)]
         + [pl.BlockSpec(memory_space=pltpu.VMEM)] * 5,
         out_specs=pl.BlockSpec(memory_space=pltpu.VMEM),
@@ -274,16 +277,18 @@
 def synthesize_kernel(x_ref, l_hbm, out_hbm, l_ref, f_ref, out_ref, sems):
     tall = 4 * SLOTS
     copies = []
-    for i in range(CLASSES + 1):
+    for i in range(PAIRED + 1):
         rows = pl.ds(i * tall, tall)
         copies.append(pltpu.make_async_copy(l_hbm.at[rows, :], l_ref.at[rows, :], sems.at[i]))
         copies[i].start()
-
-    def put(j, left, lanes, width, at):
+    r = lax.broadcasted_iota(jnp.int32, (tall, CLASSES * SLOTS), 1) % CLASSES
+
+    def put(j, group, keep, width, at):
+        left = l_ref[group * tall : (group + 1) * tall, :]
+        if keep is not None:
+            left = jnp.where(keep, left, jnp.zeros((), BF))
         summed = jnp.dot(
-            l_ref[left * tall : (left + 1) * tall, :],
-            x_ref[:, lanes : lanes + width],
-            preferred_element_type=F32,
+            left, x_ref[:, group * WIDE : group * WIDE + width], preferred_element_type=F32
         )
         for g in range(4):
             for i in range(width // 128):
@@ -291,17 +296,17 @@
                     g * SLOTS : (g + 1) * SLOTS, i * 128 : (i + 1) * 128
                 ]
 
-    for j in range(CLASSES):
-        if j in (0, PAIRED):
-            for i in range(j, PAIRED if j == 0 else CLASSES + 1):
-                copies[i].wait()
-        if j < PAIRED:
-            put(j, j, j * WIDE, WIDE, 0)
-        elif j == PAIRED:
-            for p in range(2):
-                put(j, PAIRED + p, PAIRED * WIDE, COLUMNS, p * COLUMNS)
+    for group in range(PAIRED + 1):
+        for i in WAITS.get(group, ()):
+            copies[i].wait()
+        if group == 0:
+            put(0, 0, None, WIDE, 0)
+        elif group < PAIRED:
+            put(group, group, r >= group, WIDE, 0)
+            put(CLASSES - group, group, r < group, WIDE, 0)
         else:
-            put(j, j + 1, (CLASSES - j) * WIDE, WIDE, 0)
+            put(PAIRED, group, r < PAIRED, COLUMNS, 0)
+            put(PAIRED, group, r >= PAIRED, COLUMNS, COLUMNS)
     stores = []
     for g in range(OUTS):
         part = 4 * WIDE // OUTS
@@ -310,7 +315,7 @@
         lanes = pl.ds(g * part, part)
         stores.append(
             pltpu.make_async_copy(
-                out_ref.at[:, lanes], out_hbm.at[:, lanes], sems.at[CLASSES + 1 + g]
+                out_ref.at[:, lanes], out_hbm.at[:, lanes], sems.at[PAIRED + 1 + g]
             )
         )
         stores[g].start()
@@ -332,7 +337,7 @@
             pltpu.VMEM(rows.shape, BF),
             pltpu.VMEM((4 * WIDE // 128, size, 128), F32),
             pltpu.VMEM((size, 4 * WIDE), BF),
-            pltpu.SemaphoreType.DMA((CLASSES + 5,)),
+            pltpu.SemaphoreType.DMA((PAIRED + 5,)),
         ],
         compiler_params=pltpu.CompilerParams(vmem_limit_bytes=16 * MIB),
         cost_estimate=pl.CostEstimate(

time: 160 us -> 158 us (0.988)
  Pallas kernels: 27.5 us -> 25.6 us
  transfers between devices with their start and end apart: 6 -> 6, of which waited for: 6 -> 6; matrix products, arithmetic and copies ran while one was open for 8% -> 8% of each run, Pallas kernels for 9% -> 8%
where the time goes in v2:
time: 158 us
  waiting for transfers between devices  90.6 us (57%)
  starting transfers between devices  28.6 us (18%)
  Pallas kernels  25.6 us (16%)
  other arithmetic  10.4 us (7%)
  local copies, waits for them, and re-layouts  2.38 us (2%)
    all_to_all x1, waiting for transfers between devices, local(): lax.all_to_all(fourier.reshape(SLOTS, CLASSES, 4 * WIDE), 'own', split_ax...  41 us
    all_to_all x1, waiting for transfers between devices, local(): lax.all_to_all(outgoing.reshape(SLOTS, CLASSES, PACKED), 'own', split_axi...  34.1 us
    all_to_all x1, starting transfers between devices, local(): mine = lax.all_to_all(sent, 'own', split_axis=0, concat_axis=0, tiled=True)  12.1 us
    ppermute x3, waiting for transfers between devices, local(): lax.ppermute(mine, 'grp', [(i, (i + shift) % 4) for i in range(4)])  11.5 us
    pallas_call x1, Pallas kernels, rotate(): pl.pallas_call(rotate_kernel, out_shape=pltpu.HBM((CLASSES * SLOTS, PACKE...  9.38 us
    cos x1, other arithmetic, wave_table(): jnp.cos(angles)  8.28 us
    all_to_all x1, starting transfers between devices, local(): lax.all_to_all(outgoing.reshape(SLOTS, CLASSES, PACKED), 'own', split_axi...  6.33 us
    pallas_call x1, Pallas kernels, transform(): pl.pallas_call(transform_kernel, out_shape=pltpu.HBM((COLUMNS, 4, NLON),...  5.89 us
  transfers between devices with their start and end apart: 6, of which 6 were waited for; matrix products, arithmetic and copies ran while one was open for 8% of the time, Pallas kernels for 8%

profile of v2, /device:TPU:2, one launch (start us, length us, event | category | flops | bytes accessed | tf_op | source)
XLA Modules:
  0.0 157.9 jit_solution(18083292966311090455)
XLA Ops:
  0.0 0.0 copy-start.1
  0.0 0.0 copy-start
  0.0 2.0 %scatter.1 = bf16[1152,128]{1,0:T(8,128)(2,1)} custom-call(s32[1]{0:T(128)} %bitcast.4.grp_ref, bf16[4,512,512]{2,1,0:T(8,128)(2,1)} %legendre_ref.1), custom_call_target="tpu_custom_call" | custom-call | tf_op jit(solution)/shard_map/scatter/pallas_call | solution.py:209
  2.0 12.1 %all-to-all-start.1 = ((bf16[64,9,2,128]{3,2,1,0:T(2,128)(2,1)}), bf16[64,9,2,128]{3,2,1,0:T(2,128)(2,1)S(1)}, u32[]{:S(2)}, u32[]{:S(2)}) async-start(bf16[64,9,2,128]{3,2,1,0:T(2,128)(2,1)} %bitcast.43), calls=%async_computation.1 | async-start | bytes 589824 | tf_op jit(solution)/shard_map/all_to_all | solution.py:456
  14.1 0.0 copy-done.1
  14.2 0.0 copy-done
  14.2 9.4 %rotate.1 = bf16[512,2304]{1,0:T(8,128)(2,1)} custom-call(s32[8,64]{1,0:T(8,128)S(1)} %copy-done.1, bf16[256,4608]{1,0:T(8,128)(2,1)S(1)} %bitcast.31, bf16[1,3342336]{1,0:T(2,128)(2,1)} %rot_ref.1), custom_call_target="tpu_custom_call" | custom-call | flops 4000000000 | bytes 18000000 | tf_op jit(solution)/shard_map/rotate/pallas_call | solution.py:170
  23.6 4.0 %all-to-all-done.1 = bf16[64,9,2,128]{3,2,1,0:T(2,128)(2,1)S(1)} async-done(((bf16[64,9,2,128]{3,2,1,0:T(2,128)(2,1)}), bf16[64,9,2,128]{3,2,1,0:T(2,128)(2,1)S(1)}, u32[]{:S(2)}, u32[]{:S(2)}) %all-to-all-start.1) | async-done | bytes 294944 | tf_op jit(solution)/shard_map/all_to_all | solution.py:456
  27.6 0.0 copy-start.2
  27.6 6.3 %all-to-all-start = ((bf16[64,8,2304]{2,1,0:T(8,128)(2,1)}), bf16[64,8,2304]{2,1,0:T(8,128)(2,1)S(1)}, u32[]{:S(2)}, u32[]{:S(2)}) async-start(bf16[64,8,2304]{2,1,0:T(8,128)(2,1)} %bitcast.41), calls=%async_computation | async-start | bytes 4718592 | tf_op jit(solution)/shard_map/all_to_all | solution.py:466
  33.9 0.1 copy.18
  34.0 0.1 concatenate.63
  34.1 0.1 copy.17
  34.2 0.1 concatenate.59
  34.3 0.1 copy.16
  34.4 0.1 concatenate.55
  34.6 0.1 copy.14
  34.6 0.1 concatenate.51
  34.8 0.1 add.130
  34.9 0.1 broadcast_in_dim.50
  35.0 0.1 broadcast_in_dim.53
  35.1 0.1 broadcast_in_dim.55
  35.2 0.1 add_select_fusion.1
  35.3 1.5 collective-permute-start
  36.8 1.1 collective-permute-start.1
  37.9 0.0 copy-done.2
  37.9 2.2 %collective-permute-start.2 = (bf16[64,9,2,128]{3,2,1,0:T(2,128)(2,1)S(1)}, bf16[64,9,2,128]{3,2,1,0:T(2,128)(2,1)}, u32[]{:S(2)}, u32[]{:S(2)}) collective-permute-start(bf16[64,9,2,128]{3,2,1,0:T(2,128)(2,1)S(1)} %all-to-all-done.1), channel_id=1, source_target_pairs={{0,192},{64,0},{128,64},{192,128},{1,193},{65,1},{129,65},{193,129... | collective-permute-start | bytes 884744 | tf_op jit(solution)/shard_map/ppermute | solution.py:459
  40.1 0.1 broadcast_in_dim.57
  40.2 0.1 copy.13
  40.3 0.1 stack.6
  40.4 0.1 copy.19
  40.5 0.1 stack.7
  40.6 0.6 stack.8.targets_ref
  41.2 4.0 %collective-permute-done = bf16[64,9,2,128]{3,2,1,0:T(2,128)(2,1)S(1)} collective-permute-done((bf16[64,9,2,128]{3,2,1,0:T(2,128)(2,1)S(1)}, bf16[64,9,2,128]{3,2,1,0:T(2,128)(2,1)S(1)}, u32[]{:S(2)}, u32[]{:S(2)}) %collective-permute-start) | collective-permute-done | bytes 294944 | tf_op jit(solution)/shard_map/ppermute | solution.py:459
  45.2 0.0 copy-start.4
  45.2 3.0 %collective-permute-done.1 = bf16[64,9,2,128]{3,2,1,0:T(2,128)(2,1)S(1)} collective-permute-done((bf16[64,9,2,128]{3,2,1,0:T(2,128)(2,1)S(1)}, bf16[64,9,2,128]{3,2,1,0:T(2,128)(2,1)S(1)}, u32[]{:S(2)}, u32[]{:S(2)}) %collective-permute-start.1) | collective-permute-done | bytes 294944 | tf_op jit(solution)/shard_map/ppermute | solution.py:459
  48.2 0.0 copy-start.5
  48.2 4.6 %collective-permute-done.2 = bf16[64,9,2,128]{3,2,1,0:T(2,128)(2,1)} collective-permute-done((bf16[64,9,2,128]{3,2,1,0:T(2,128)(2,1)S(1)}, bf16[64,9,2,128]{3,2,1,0:T(2,128)(2,1)}, u32[]{:S(2)}, u32[]{:S(2)}) %collective-permute-start.2) | collective-permute-done | bytes 294944 | tf_op jit(solution)/shard_map/ppermute | solution.py:459
  52.8 0.0 copy-done.4
  52.8 0.0 copy-done.5
  52.8 4.0 %legendre.1.l_hbm = bf16[1280,512]{1,0:T(8,128)(2,1)} custom-call(s32[1]{0:T(128)} %bitcast.4.grp_ref, s32[8,512]{1,0:T(8,128)} %stack.8.targets_ref, bf16[1152,128]{1,0:T(8,128)(2,1)} %bitcast.44, bf16[1152,128]{1,0:T(8,128)(2,1)} %bitcast.46, bf16[1152,128]{1,0:T(8,128)(2,1)} %bitcast.47, bf16[1152,128]{1,0:T(8,128)(2,1)} %bitcast.18.refs_3_), custom_call_target="tpu_custom_call" | custom-call | flops 1000000000 | bytes 4000000 | tf_op jit(solution)/shard_map/legendre/pallas_call | solution.py:261
  56.8 34.1 %all-to-all-done = bf16[64,8,2304]{2,1,0:T(8,128)(2,1)S(1)} async-done(((bf16[64,8,2304]{2,1,0:T(8,128)(2,1)}), bf16[64,8,2304]{2,1,0:T(8,128)(2,1)S(1)}, u32[]{:S(2)}, u32[]{:S(2)}) %all-to-all-start) | async-done | bytes 2359328 | tf_op jit(solution)/shard_map/all_to_all | solution.py:466
  90.8 4.3 %synthesize.1 = bf16[512,2048]{1,0:T(8,128)(2,1)} custom-call(bf16[512,2304]{1,0:T(8,128)(2,1)S(1)} %bitcast.32, bf16[1280,512]{1,0:T(8,128)(2,1)} %legendre.1.l_hbm), custom_call_target="tpu_custom_call" | custom-call | flops 2000000000 | bytes 7000000 | tf_op jit(solution)/shard_map/synthesize/pallas_call | solution.py:328
  95.2 0.0 copy-start.3
  95.2 5.3 %all-to-all-start.2 = ((bf16[64,8,2048]{2,1,0:T(8,128)(2,1)}), bf16[64,8,2048]{2,1,0:T(8,128)(2,1)S(1)}, u32[]{:S(2)}, u32[]{:S(2)}) async-start(bf16[64,8,2048]{2,1,0:T(8,128)(2,1)} %bitcast.42), calls=%async_computation.2 | async-start | bytes 4194304 | tf_op jit(solution)/shard_map/all_to_all | solution.py:470
  100.5 0.0 copy-done.3
  100.6 0.1 copy.20.order_ref
  100.7 8.3 %fusion.8 = (f32[512,1024]{1,0:T(8,128)S(1)}, f32[512,1024]{1,0:T(8,128)S(1)}) fusion(s32[512]{0:T(512)S(1)} %fusion.13), kind=kLoop, calls=%fused_computation.12 | loop fusion | flops 7340032 | bytes 4196352 | tf_op jit(solution)/shard_map/cos | solution.py:434
  109.0 1.9 %fusion.w_hbm = bf16[1024,1024]{1,0:T(8,128)(2,1)} fusion(f32[512,1024]{1,0:T(8,128)S(1)} %get-tuple-element.10, f32[512,1024]{1,0:T(8,128)S(1)} %get-tuple-element.9), kind=kLoop, calls=%fused_computation.1 | loop fusion | flops 3145728 | bytes 6291456 | tf_op jit(solution)/shard_map/convert_element_type | solution.py:434
  110.9 41.0 %all-to-all-done.2 = bf16[64,8,2048]{2,1,0:T(8,128)(2,1)S(1)} async-done(((bf16[64,8,2048]{2,1,0:T(8,128)(2,1)}), bf16[64,8,2048]{2,1,0:T(8,128)(2,1)S(1)}, u32[]{:S(2)}, u32[]{:S(2)}) %all-to-all-start.2) | async-done | bytes 2097184 | tf_op jit(solution)/shard_map/all_to_all | solution.py:470
  151.9 5.9 %transform.1 = bf16[256,4,1024]{2,1,0:T(4,128)(2,1)} custom-call(s32[256,1]{1,0:T(8,128)S(1)} %copy.20.order_ref, bf16[512,2048]{1,0:T(8,128)(2,1)S(1)} %bitcast.33, bf16[1024,1024]{1,0:T(8,128)(2,1)} %fusion.w_hbm), custom_call_target="tpu_custom_call" | custom-call | flops 2000000000 | bytes 7000000 | tf_op jit(solution)/shard_map/transform/pallas_call | solution.py:405
  (24 shorter events, 0.2 us)
Async XLA Ops:
  0.0 14.1 %copy-start.1 = (s32[8,64]{1,0:T(8,128)S(1)}, s32[8,64]{1,0:T(8,128)}, u32[]{:S(2)}) copy-start(s32[8,64]{1,0:T(8,128)} %deg_ref.1) | copy-start | bytes 6148
  0.0 14.2 %copy-start = (bf16[1,256,4608]{2,1,0:T(8,128)(2,1)S(1)}, bf16[1,256,4608]{2,1,0:T(8,128)(2,1)}, u32[]{:S(2)}) copy-start(bf16[1,256,4608]{2,1,0:T(8,128)(2,1)} %param.5) | copy-start | bytes 7077892
  2.0 25.5 %all-to-all-start.1 = ((bf16[64,9,2,128]{3,2,1,0:T(2,128)(2,1)}), bf16[64,9,2,128]{3,2,1,0:T(2,128)(2,1)S(1)}, u32[]{:S(2)}, u32[]{:S(2)}) async-start(bf16[64,9,2,128]{3,2,1,0:T(2,128)(2,1)} %bitcast.43), calls=%async_computation.1 | async-start | bytes 589824 | tf_op jit(solution)/shard_map/all_to_all | solution.py:456
  27.6 10.4 %copy-start.2 = (bf16[64,9,2,128]{3,2,1,0:T(2,128)(2,1)}, bf16[64,9,2,128]{3,2,1,0:T(2,128)(2,1)S(1)}, u32[]{:S(2)}) copy-start(bf16[64,9,2,128]{3,2,1,0:T(2,128)(2,1)S(1)} %all-to-all-done.1) | copy-start | bytes 884740
  27.6 63.3 %all-to-all-start = ((bf16[64,8,2304]{2,1,0:T(8,128)(2,1)}), bf16[64,8,2304]{2,1,0:T(8,128)(2,1)S(1)}, u32[]{:S(2)}, u32[]{:S(2)}) async-start(bf16[64,8,2304]{2,1,0:T(8,128)(2,1)} %bitcast.41), calls=%async_computation | async-start | bytes 4718592 | tf_op jit(solution)/shard_map/all_to_all | solution.py:466
  35.3 9.9 %collective-permute-start = (bf16[64,9,2,128]{3,2,1,0:T(2,128)(2,1)S(1)}, bf16[64,9,2,128]{3,2,1,0:T(2,128)(2,1)S(1)}, u32[]{:S(2)}, u32[]{:S(2)}) collective-permute-start(bf16[64,9,2,128]{3,2,1,0:T(2,128)(2,1)S(1)} %all-to-all-done.1), channel_id=1, source_target_pairs={{0,64},{64,128},{128,192},{192,0},{1,65},{65,129},{129,193},{193,1... | collective-permute-start | bytes 884744 | tf_op jit(solution)/shard_map/ppermute | solution.py:459
  36.8 11.4 %collective-permute-start.1 = (bf16[64,9,2,128]{3,2,1,0:T(2,128)(2,1)S(1)}, bf16[64,9,2,128]{3,2,1,0:T(2,128)(2,1)S(1)}, u32[]{:S(2)}, u32[]{:S(2)}) collective-permute-start(bf16[64,9,2,128]{3,2,1,0:T(2,128)(2,1)S(1)} %all-to-all-done.1), channel_id=1, source_target_pairs={{0,128},{64,192},{128,0},{192,64},{1,129},{65,193},{129,1},{193,65... | collective-permute-start | bytes 884744 | tf_op jit(solution)/shard_map/ppermute | solution.py:459
  37.9 14.8 %collective-permute-start.2 = (bf16[64,9,2,128]{3,2,1,0:T(2,128)(2,1)S(1)}, bf16[64,9,2,128]{3,2,1,0:T(2,128)(2,1)}, u32[]{:S(2)}, u32[]{:S(2)}) collective-permute-start(bf16[64,9,2,128]{3,2,1,0:T(2,128)(2,1)S(1)} %all-to-all-done.1), channel_id=1, source_target_pairs={{0,192},{64,0},{128,64},{192,128},{1,193},{65,1},{129,65},{193,129... | collective-permute-start | bytes 884744 | tf_op jit(solution)/shard_map/ppermute | solution.py:459
  45.2 7.6 %copy-start.4 = (bf16[64,9,2,128]{3,2,1,0:T(2,128)(2,1)}, bf16[64,9,2,128]{3,2,1,0:T(2,128)(2,1)S(1)}, u32[]{:S(2)}) copy-start(bf16[64,9,2,128]{3,2,1,0:T(2,128)(2,1)S(1)} %collective-permute-done) | copy-start | bytes 884740
  48.2 4.6 %copy-start.5 = (bf16[64,9,2,128]{3,2,1,0:T(2,128)(2,1)}, bf16[64,9,2,128]{3,2,1,0:T(2,128)(2,1)S(1)}, u32[]{:S(2)}) copy-start(bf16[64,9,2,128]{3,2,1,0:T(2,128)(2,1)S(1)} %collective-permute-done.1) | copy-start | bytes 884740
  95.2 5.4 %copy-start.3 = (s32[256]{0:T(256)S(1)}, s32[256]{0:T(256)}, u32[]{:S(2)}) copy-start(s32[256]{0:T(256)} %param.9) | copy-start | bytes 3076
  95.2 56.7 %all-to-all-start.2 = ((bf16[64,8,2048]{2,1,0:T(8,128)(2,1)}), bf16[64,8,2048]{2,1,0:T(8,128)(2,1)S(1)}, u32[]{:S(2)}, u32[]{:S(2)}) async-start(bf16[64,8,2048]{2,1,0:T(8,128)(2,1)} %bitcast.42), calls=%async_computation.2 | async-start | bytes 4194304 | tf_op jit(solution)/shard_map/all_to_all | solution.py:470
